TPU v7x, 32 devices: a whole 2x2x4 slice. The times are simulated.
32 devices in a mesh: replica: 2 (over y), fsdp: 4 (over z), tensor: 4 (over x, core).
Axes of the slice: x: 2, y: 2, z: 4, core: 2. Of those that a mesh axis runs over, the one named last changes fastest.
Arguments:
- tokens: bfloat16 [24576, 1024], P(('replica', 'fsdp', 'tensor')), may hold values from -6 to 6
- ln1_gain: float32 [1024], P(('fsdp', 'tensor')), may hold values from 0.5 to 1.5
- ln1_bias: float32 [1024], P(('fsdp', 'tensor')), may hold values from -3 to 3
- qkv_weight: bfloat16 [1024, 3, 1024], P('fsdp', None, 'tensor'), may hold values from -0.1875 to 0.1875
- qv_bias: bfloat16 [2, 16, 64], P(None, 'tensor', 'fsdp'), may hold values from -3 to 3
- out_weight: bfloat16 [1024, 1024], P('tensor', 'fsdp'), may hold values from -0.75 to 0.75
- out_bias: float32 [1024], P(('fsdp', 'tensor')), may hold values from -3 to 3
- ln2_gain: float32 [1024], P(('fsdp', 'tensor')), may hold values from 0.5 to 1.5
- ln2_bias: float32 [1024], P(('fsdp', 'tensor')), may hold values from -3 to 3
- fc_weight: bfloat16 [1024, 4096], P('fsdp', 'tensor'), may hold values from -0.1875 to 0.1875
- fc_bias: bfloat16 [64, 64], P('tensor', 'fsdp'), may hold values from -3 to 3
- proj_weight: bfloat16 [4096, 1024], P('tensor', 'fsdp'), may hold values from -0.09375 to 0.09375
- proj_bias: float32 [1024], P(('fsdp', 'tensor')), may hold values from -3 to 3
- out_grad: bfloat16 [24576, 1024], P(('replica', 'fsdp', 'tensor')), may hold values from -6 to 6
Outputs:
- output: float32 [24576, 1024], P(('replica', 'fsdp', 'tensor'))
- input_grad: float32 [24576, 1024], P(('replica', 'fsdp', 'tensor'))
- grad_ln1_gain: float32 [1024], P(('fsdp', 'tensor'))
- grad_ln1_bias: float32 [1024], P(('fsdp', 'tensor'))
- grad_qkv_weight: float32 [1024, 3, 1024], P('fsdp', None, 'tensor')
- grad_qv_bias: float32 [2, 16, 64], P(None, 'tensor', 'fsdp')
- grad_out_weight: float32 [1024, 1024], P('tensor', 'fsdp')
- grad_out_bias: float32 [1024], P(('fsdp', 'tensor'))
- grad_ln2_gain: float32 [1024], P(('fsdp', 'tensor'))
- grad_ln2_bias: float32 [1024], P(('fsdp', 'tensor'))
- grad_fc_weight: float32 [1024, 4096], P('fsdp', 'tensor')
- grad_fc_bias: float32 [64, 64], P('tensor', 'fsdp')
- grad_proj_weight: float32 [4096, 1024], P('tensor', 'fsdp')
- grad_proj_bias: float32 [1024], P(('fsdp', 'tensor'))
All inputs are finite; a program needn't handle non-finite values.
Results may differ from a plain program's by a relative error of at most 0.014.
Values may be sent and summed in bfloat16 or wider, within the bound.
A program may use at most 192 MiB of HBM per device.

v0:
```python
import jax
import jax.numpy as jnp
from jax import lax
from jax.sharding import PartitionSpec as P

HD = 64
LEN = 1024


EPS = 1e-05
NEG = -1e30


def layer_norm(values, gain, bias):
    center = values - jnp.mean(values, -1, keepdims=True)
    spread = jnp.mean(center * center, -1, keepdims=True)
    return center * lax.rsqrt(spread + EPS) * gain + bias


def gelu_tanh(values):
    return jax.nn.gelu(values, approximate=True)


def unpack(gathered):
    qkv_full, qv_full, out_full, fc_full, fcb_full, proj_full = gathered
    width = qkv_full.shape[2]
    joined = qkv_full.reshape(qkv_full.shape[0], 3 * width)
    bias_row = jnp.concatenate(
        [
            qv_full[0].reshape(width).astype(jnp.float32),
            jnp.zeros((width,), jnp.float32),
            qv_full[1].reshape(width).astype(jnp.float32),
        ]
    )
    return (
        joined,
        bias_row,
        out_full,
        fc_full,
        fcb_full.reshape(-1).astype(jnp.float32),
        proj_full,
    )


def masked_scores(query_block, keys, start, block_rows):
    scores = jnp.einsum(
        "qhd,khd->hqk", query_block, keys, preferred_element_type=jnp.float32
    ) * HD ** (-0.5)
    allowed = (start + jnp.arange(block_rows, dtype=jnp.int32))[:, None] >= jnp.arange(
        LEN, dtype=jnp.int32
    )[None, :]
    return jnp.where(allowed[None], scores, NEG)


def spread_rows(local, project):
    return (project(lax.all_gather(local, "tensor", axis=0, tiled=True), jnp.int32(0)), local)


def gather_sum(left, right):
    return lax.psum_scatter(
        jnp.dot(left, right, preferred_element_type=jnp.float32),
        "tensor",
        scatter_dimension=0,
        tiled=True,
    )


def back_rows(local_grad, left, weight):

    def add_piece(carry, piece, start):
        grad_weight = lax.dot_general(
            left, piece, (((0,), (0,)), ((), ())), preferred_element_type=jnp.float32
        )
        part = lax.dot_general(
            piece, weight, (((1,), (1,)), ((), ())), preferred_element_type=jnp.float32
        )
        return (grad_weight, part)

    init = (
        jnp.zeros((left.shape[1], weight.shape[1]), jnp.float32),
        jnp.zeros((left.shape[0], weight.shape[0]), jnp.float32),
    )
    return add_piece(init, lax.all_gather(local_grad, "tensor", axis=0, tiled=True), jnp.int32(0))


def back_normed(kept, grad, weight):

    def add_piece(total, piece, start):
        return lax.dot_general(
            piece, grad, (((0,), (0,)), ((), ())), preferred_element_type=jnp.float32
        )

    grad_weight = add_piece(
        jnp.zeros((kept.shape[1], grad.shape[1]), jnp.float32),
        lax.all_gather(kept, "tensor", axis=0, tiled=True),
        jnp.int32(0),
    )
    return (
        grad_weight,
        lax.psum_scatter(
            lax.dot_general(
                grad, weight, (((1,), (1,)), ((), ())), preferred_element_type=jnp.float32
            ),
            "tensor",
            scatter_dimension=0,
            tiled=True,
        ),
    )


def on_device(
    tokens,
    ln1_gain,
    ln1_bias,
    qkv_weight,
    qv_bias,
    out_weight,
    out_bias,
    ln2_gain,
    ln2_bias,
    fc_weight,
    fc_bias,
    proj_weight,
    proj_bias,
    out_grad,
):
    rows = tokens.shape[0]
    group_rows = rows * lax.axis_size("tensor")
    seqs = group_rows // LEN
    block_rows = min(512, LEN)
    blocks = LEN // block_rows
    scale = HD ** (-0.5)
    gain_one, bias_one, gain_two, bias_two, bias_out, bias_proj = (
        lax.all_gather(ln1_gain, ("fsdp", "tensor"), axis=0, tiled=True),
        lax.all_gather(ln1_bias, ("fsdp", "tensor"), axis=0, tiled=True),
        lax.all_gather(ln2_gain, ("fsdp", "tensor"), axis=0, tiled=True),
        lax.all_gather(ln2_bias, ("fsdp", "tensor"), axis=0, tiled=True),
        lax.all_gather(out_bias, ("fsdp", "tensor"), axis=0, tiled=True),
        lax.all_gather(proj_bias, ("fsdp", "tensor"), axis=0, tiled=True),
    )
    weight_set = (qkv_weight, qv_bias, out_weight, fc_weight, fc_bias, proj_weight)
    gathered = (
        lax.all_gather(weight_set[0], "fsdp", axis=0, tiled=True),
        lax.all_gather(weight_set[1], "fsdp", axis=2, tiled=True),
        lax.all_gather(weight_set[2], "fsdp", axis=1, tiled=True),
        lax.all_gather(weight_set[3], "fsdp", axis=0, tiled=True),
        lax.all_gather(weight_set[4], "fsdp", axis=1, tiled=True),
        lax.all_gather(weight_set[5], "fsdp", axis=1, tiled=True),
    )
    joined, bias_row, out_full, fc_full, fcb_full, proj_full = unpack(gathered)
    width = out_full.shape[0]
    local_heads = width // HD
    inputs = tokens.astype(jnp.float32)
    normed_one = layer_norm(inputs, gain_one, bias_one).astype(jnp.bfloat16)

    def project_qkv(piece, start):
        return (jnp.dot(piece, joined, preferred_element_type=jnp.float32) + bias_row).astype(
            jnp.bfloat16
        )

    qkv, kept_one = spread_rows(normed_one, project_qkv)
    grid_shape = (seqs, LEN, local_heads, HD)
    query = qkv[:, :width].reshape(grid_shape)
    keys = qkv[:, width : 2 * width].reshape(grid_shape)
    values = qkv[:, 2 * width :].reshape(grid_shape)
    starts = jnp.arange(blocks, dtype=jnp.int32) * block_rows

    def attend_sequence(item):
        query_seq, keys_seq, values_seq = item

        def one_block(inner):
            query_block, start = inner
            scores = masked_scores(query_block, keys_seq, start, block_rows)
            top = jnp.max(scores, -1, keepdims=True)
            expo = jnp.exp(scores - top)
            total = jnp.sum(expo, -1, keepdims=True)
            probs = (expo / total).astype(jnp.bfloat16)
            result = jnp.einsum(
                "hqk,khd->qhd", probs, values_seq, preferred_element_type=jnp.float32
            ).astype(jnp.bfloat16)
            return (result, (top + jnp.log(total))[..., 0])

        result, log_total = lax.map(
            one_block, (query_seq.reshape(blocks, block_rows, local_heads, HD), starts)
        )
        return (result.reshape(LEN, width), log_total)

    attended, log_totals = lax.map(attend_sequence, (query, keys, values))
    attended = attended.reshape(group_rows, width)
    middle = inputs + (gather_sum(attended, out_full) + bias_out)
    normed_two = layer_norm(middle, gain_two, bias_two).astype(jnp.bfloat16)

    def project_fc(piece, start):
        return jnp.dot(piece, fc_full, preferred_element_type=jnp.float32) + fcb_full

    before, kept_two = spread_rows(normed_two, project_fc)
    activated = gelu_tanh(before).astype(jnp.bfloat16)
    output = middle + gather_sum(activated, proj_full) + bias_proj
    again = (
        lax.all_gather(weight_set[0], "fsdp", axis=0, tiled=True),
        lax.all_gather(weight_set[1], "fsdp", axis=2, tiled=True),
        lax.all_gather(weight_set[2], "fsdp", axis=1, tiled=True),
        lax.all_gather(weight_set[3], "fsdp", axis=0, tiled=True),
        lax.all_gather(weight_set[4], "fsdp", axis=1, tiled=True),
        lax.all_gather(weight_set[5], "fsdp", axis=1, tiled=True),
    )
    joined, bias_row, out_full, fc_full, fcb_full, proj_full = unpack(again)
    grad_proj, grad_act = back_rows(out_grad, activated, proj_full)
    grad_proj_bias = jnp.sum(out_grad, 0, dtype=jnp.float32)
    gelu_pull = jax.vjp(gelu_tanh, before)[1]
    grad_pre = gelu_pull(grad_act)[0].astype(jnp.bfloat16)
    grad_fc_bias = jnp.sum(grad_pre, 0, dtype=jnp.float32)
    grad_fc, grad_normed_two = back_normed(kept_two, grad_pre, fc_full)
    norm_pull_two = jax.vjp(layer_norm, middle, gain_two, bias_two)[1]
    grad_middle_part, grad_gain_two, grad_bias_two = norm_pull_two(grad_normed_two)
    grad_middle = out_grad.astype(jnp.float32) + grad_middle_part
    grad_branch = grad_middle.astype(jnp.bfloat16)
    grad_out_bias = jnp.sum(grad_branch, 0, dtype=jnp.float32)
    grad_out, grad_attended = back_rows(grad_branch, attended, out_full)
    grad_attended = grad_attended.astype(jnp.bfloat16).reshape(grid_shape)

    def attend_back_sequence(item):
        query_seq, keys_seq, values_seq, grad_seq, log_seq = item

        def one_block(carry, inner):
            grad_keys, grad_values = carry
            query_block, grad_block, total_block, start = inner
            scores = masked_scores(query_block, keys_seq, start, block_rows)
            probs = jnp.exp(scores - total_block[:, :, None])
            grad_values = grad_values + jnp.einsum(
                "hqk,qhd->khd",
                probs.astype(jnp.bfloat16),
                grad_block,
                preferred_element_type=jnp.float32,
            )
            grad_probs = jnp.einsum(
                "qhd,khd->hqk", grad_block, values_seq, preferred_element_type=jnp.float32
            )
            grad_scores = (
                probs * (grad_probs - jnp.sum(probs * grad_probs, -1, keepdims=True))
            ).astype(jnp.bfloat16)
            grad_query = (
                jnp.einsum(
                    "hqk,khd->qhd", grad_scores, keys_seq, preferred_element_type=jnp.float32
                )
                * scale
            )
            grad_keys = (
                grad_keys
                + jnp.einsum(
                    "hqk,qhd->khd", grad_scores, query_block, preferred_element_type=jnp.float32
                )
                * scale
            )
            return ((grad_keys, grad_values), grad_query)

        zeros = jnp.zeros((LEN, local_heads, HD), jnp.float32)
        block_shape = (blocks, block_rows, local_heads, HD)
        (grad_keys, grad_values), grad_query = lax.scan(
            one_block,
            (zeros, zeros),
            (query_seq.reshape(block_shape), grad_seq.reshape(block_shape), log_seq, starts),
        )
        return jnp.concatenate(
            [
                grad_query.reshape(LEN, width),
                grad_keys.reshape(LEN, width),
                grad_values.reshape(LEN, width),
            ],
            -1,
        ).astype(jnp.bfloat16)

    grad_qkv = lax.map(
        attend_back_sequence, (query, keys, values, grad_attended, log_totals)
    ).reshape(group_rows, 3 * width)
    qkv_sums = jnp.sum(grad_qkv, 0, dtype=jnp.float32)
    grad_qv = jnp.stack([qkv_sums[:width], qkv_sums[2 * width :]]).reshape(2, local_heads, HD)
    grad_joined, grad_normed_one = back_normed(kept_one, grad_qkv, joined)
    grad_joined = grad_joined.reshape(grad_joined.shape[0], 3, width)
    norm_pull_one = jax.vjp(layer_norm, inputs, gain_one, bias_one)[1]
    grad_input_part, grad_gain_one, grad_bias_one = norm_pull_one(grad_normed_one)
    input_grad = grad_middle + grad_input_part
    fsdp_sums = (
        lax.psum_scatter(
            grad_joined.astype(jnp.bfloat16), "fsdp", scatter_dimension=0, tiled=True
        ).astype(jnp.float32),
        lax.psum_scatter(
            grad_qv.astype(jnp.bfloat16), "fsdp", scatter_dimension=2, tiled=True
        ).astype(jnp.float32),
        lax.psum_scatter(
            grad_out.astype(jnp.bfloat16), "fsdp", scatter_dimension=1, tiled=True
        ).astype(jnp.float32),
        lax.psum_scatter(
            grad_fc.astype(jnp.bfloat16), "fsdp", scatter_dimension=0, tiled=True
        ).astype(jnp.float32),
        lax.psum_scatter(
            grad_fc_bias.reshape(-1, HD).astype(jnp.bfloat16),
            "fsdp",
            scatter_dimension=1,
            tiled=True,
        ).astype(jnp.float32),
        lax.psum_scatter(
            grad_proj.astype(jnp.bfloat16), "fsdp", scatter_dimension=1, tiled=True
        ).astype(jnp.float32),
    )
    vector_sums = (
        lax.psum_scatter(grad_gain_one, ("fsdp", "tensor"), scatter_dimension=0, tiled=True),
        lax.psum_scatter(grad_bias_one, ("fsdp", "tensor"), scatter_dimension=0, tiled=True),
        lax.psum_scatter(grad_out_bias, ("fsdp", "tensor"), scatter_dimension=0, tiled=True),
        lax.psum_scatter(grad_gain_two, ("fsdp", "tensor"), scatter_dimension=0, tiled=True),
        lax.psum_scatter(grad_bias_two, ("fsdp", "tensor"), scatter_dimension=0, tiled=True),
        lax.psum_scatter(grad_proj_bias, ("fsdp", "tensor"), scatter_dimension=0, tiled=True),
    )
    totals = (
        lax.psum(fsdp_sums[0].astype(jnp.bfloat16), "replica").astype(jnp.float32),
        lax.psum(fsdp_sums[1].astype(jnp.bfloat16), "replica").astype(jnp.float32),
        lax.psum(fsdp_sums[2].astype(jnp.bfloat16), "replica").astype(jnp.float32),
        lax.psum(fsdp_sums[3].astype(jnp.bfloat16), "replica").astype(jnp.float32),
        lax.psum(fsdp_sums[4].astype(jnp.bfloat16), "replica").astype(jnp.float32),
        lax.psum(fsdp_sums[5].astype(jnp.bfloat16), "replica").astype(jnp.float32),
        lax.psum(vector_sums[0].astype(jnp.bfloat16), "replica").astype(jnp.float32),
        lax.psum(vector_sums[1].astype(jnp.bfloat16), "replica").astype(jnp.float32),
        lax.psum(vector_sums[2].astype(jnp.bfloat16), "replica").astype(jnp.float32),
        lax.psum(vector_sums[3].astype(jnp.bfloat16), "replica").astype(jnp.float32),
        lax.psum(vector_sums[4].astype(jnp.bfloat16), "replica").astype(jnp.float32),
        lax.psum(vector_sums[5].astype(jnp.bfloat16), "replica").astype(jnp.float32),
    )
    return (
        output,
        input_grad,
        totals[6],
        totals[7],
        totals[0],
        totals[1],
        totals[2],
        totals[8],
        totals[9],
        totals[10],
        totals[3],
        totals[4],
        totals[5],
        totals[11],
    )


def solution(mesh):
    placed = (
        P(("replica", "fsdp", "tensor"), None),
        P(("fsdp", "tensor")),
        P(("fsdp", "tensor")),
        P("fsdp", None, "tensor"),
        P(None, "tensor", "fsdp"),
        P("tensor", "fsdp"),
        P(("fsdp", "tensor")),
        P(("fsdp", "tensor")),
        P(("fsdp", "tensor")),
        P("fsdp", "tensor"),
        P("tensor", "fsdp"),
        P("tensor", "fsdp"),
        P(("fsdp", "tensor")),
        P(("replica", "fsdp", "tensor"), None),
    )
    return jax.shard_map(
        on_device,
        mesh=mesh,
        in_specs=placed,
        out_specs=(
            P(("replica", "fsdp", "tensor"), None),
            P(("replica", "fsdp", "tensor"), None),
            P(("fsdp", "tensor")),
            P(("fsdp", "tensor")),
            P("fsdp", None, "tensor"),
            P(None, "tensor", "fsdp"),
            P("tensor", "fsdp"),
            P(("fsdp", "tensor")),
            P(("fsdp", "tensor")),
            P(("fsdp", "tensor")),
            P("fsdp", "tensor"),
            P("tensor", "fsdp"),
            P("tensor", "fsdp"),
            P(("fsdp", "tensor")),
        ),
        check_vma=False,
    )
```

profile of v0, /device:TPU:0, one launch (start us, length us, event | category | flops | bytes accessed | tf_op | source)
XLA Modules:
  0.0 1240.5 jit_solution(8017026321018766564)
XLA Ops:
  15.5 64.3 %all-reduce.13 = (f32[1024]{0:T(1024)S(1)}, f32[1024]{0:T(1024)S(1)}, f32[1024]{0:T(1024)}, f32[1024]{0:T(1024)}, f32[1024]{0:T(1024)}) all-reduce(f32[1024]{0:T(1024)S(1)} %dynamic-update-slice.1, f32[1024]{0:T(1024)S(1)} %dynamic-update-slice, ...), channel_id=1, replica_groups=mesh['replica'=2,'fsdp'=4,'tensor'=4] {'fsdp','tensor'}, use_global_device_ids=true, to_apply=%add.1 | all-reduce | flops 5120 | bytes 40960
  85.3 13.1 %all_gather.58 = bf16[2,4,64]{1,0,2:T(2,128)(2,1)S(1)} all-gather(bf16[2,4,16]{1,0,2:T(2,128)(2,1)S(1)} %copy.131), channel_id=1, replica_groups=mesh['replica'=2,'fsdp'=4,'tensor'=4] {'fsdp'}, dimensions={2}, use_global_device_ids=true | all-gather | bytes 1280 | tf_op jit(solution)/shard_map/all_gather | solution.py:144
  98.9 15.6 %all_gather.59 = bf16[256,1024]{1,0:T(8,128)(2,1)} all-gather(bf16[256,256]{1,0:T(8,128)(2,1)S(1)} %copy-done.25), channel_id=1, replica_groups=mesh['replica'=2,'fsdp'=4,'tensor'=4] {'fsdp'}, dimensions={1}, use_global_device_ids=true | all-gather | bytes 655360 | tf_op jit(solution)/shard_map/all_gather | solution.py:145
  114.5 14.4 %all-gather.8.cloned.1.call-done = bf16[3072,1024]{1,0:T(8,128)(2,1)} async-done(((bf16[768,1024]{1,0:T(8,128)(2,1)}), bf16[3072,1024]{1,0:T(8,128)(2,1)}) %all-gather.8.cloned.1.call-update) | async-done | bytes 6291472 | tf_op jit(solution)/shard_map/all_gather | solution.py:56
  164.7 78.7 %while.54 = (s32[]{:T(128)}, bf16[3,1024,256]{2,1,0:T(8,128)(2,1)}, f32[3,2,4,512]{3,2,1,0:T(4,128)S(1)}, bf16[3,1024,4,64]{1,3,2,0:T(8,128)(2,1)}, bf16[3,1024,...) while((s32[]{:T(128)}, bf16[3,1024,256]{2,1,0:T(8,128)(2,1)}, ...), condition=%wide.region_7.8_spmd.clone, body=%wide.region_2.7_spmd.clone.sunk | while | flops 562690560 | bytes 43618704 | solution.py:188
  168.2 19.5 %while.57 = (s32[]{:T(128)}, bf16[2,512,4,64]{1,3,2,0:T(8,128)(2,1)}, f32[2,4,512]{2,1,0:T(4,128)S(1)}, s32[2]{0:T(128)S(1)}, bf16[2,512,4,64]{1,3,2,0:T(8,128)(...) while((s32[]{:T(128)}, bf16[2,512,4,64]{1,3,2,0:T(8,128)(2,1)}, ...), condition=%wide.region_6.6_spmd, body=%wide.region_3.5_spmd.sunk | while | flops 562690560 | bytes 35197132 | solution.py:183
  194.3 19.5 %while.57 = (s32[]{:T(128)}, bf16[2,512,4,64]{1,3,2,0:T(8,128)(2,1)}, f32[2,4,512]{2,1,0:T(4,128)S(1)}, s32[2]{0:T(128)S(1)}, bf16[2,512,4,64]{1,3,2,0:T(8,128)(...) while((s32[]{:T(128)}, bf16[2,512,4,64]{1,3,2,0:T(8,128)(2,1)}, ...), condition=%wide.region_6.6_spmd, body=%wide.region_3.5_spmd.sunk | while | flops 562690560 | bytes 35197132 | solution.py:183
  220.4 19.5 %while.57 = (s32[]{:T(128)}, bf16[2,512,4,64]{1,3,2,0:T(8,128)(2,1)}, f32[2,4,512]{2,1,0:T(4,128)S(1)}, s32[2]{0:T(128)S(1)}, bf16[2,512,4,64]{1,3,2,0:T(8,128)(...) while((s32[]{:T(128)}, bf16[2,512,4,64]{1,3,2,0:T(8,128)(2,1)}, ...), condition=%wide.region_6.6_spmd, body=%wide.region_3.5_spmd.sunk | while | flops 562690560 | bytes 35197132 | solution.py:183
  252.5 99.1 %reduce-scatter.15.cloned.1.call-done = f32[768,1024]{1,0:T(8,128)} async-done(((f32[3072,1024]{1,0:T(8,128)}), f32[768,1024]{1,0:T(8,128)}) %reduce-scatter.15.cloned.1.call-update) | async-done | bytes 3145744 | tf_op jit(solution)/shard_map/reduce_scatter | solution.py:60
  358.4 13.6 %all_gather.65 = bf16[16,64]{0,1:T(8,128)(2,1)S(1)} all-gather(bf16[16,16]{0,1:T(8,128)(2,1)S(1)} %copy.141), channel_id=1, replica_groups=mesh['replica'=2,'fsdp'=4,'tensor'=4] {'fsdp'}, dimensions={1}, use_global_device_ids=true | all-gather | bytes 2560 | tf_op jit(solution)/shard_map/all_gather | solution.py:147
  372.1 26.7 %all-gather.14.cloned.1.call-done = bf16[1024,1024]{1,0:T(8,128)(2,1)} async-done(((bf16[256,1024]{1,0:T(8,128)(2,1)}), bf16[1024,1024]{1,0:T(8,128)(2,1)}) %all-gather.14.cloned.1.call-update) | async-done | bytes 2097168 | tf_op jit(solution)/shard_map/all_gather | solution.py:146
  398.8 47.2 %all-gather.12.cloned.1.call-done = bf16[3072,1024]{1,0:T(8,128)(2,1)} async-done(((bf16[768,1024]{1,0:T(8,128)(2,1)}), bf16[3072,1024]{1,0:T(8,128)(2,1)}) %all-gather.12.cloned.1.call-update) | async-done | bytes 6291472 | tf_op jit(solution)/shard_map/all_gather | solution.py:56
  446.0 12.1 fusion.85
  458.1 35.7 %all-gather.16.cloned.1.call-done = bf16[1024,1024]{1,0:T(8,128)(2,1)} async-done(((bf16[1024,256]{1,0:T(8,128)(2,1)}), bf16[1024,1024]{1,0:T(8,128)(2,1)}) %all-gather.16.cloned.1.call-update) | async-done | bytes 2097168 | tf_op jit(solution)/shard_map/all_gather | solution.py:148
  493.7 46.1 %all-gather.18.cloned.1.call-done = bf16[3072,1024]{1,0:T(8,128)(2,1)} async-done(((bf16[768,1024]{1,0:T(8,128)(2,1)}), bf16[3072,1024]{1,0:T(8,128)(2,1)}) %all-gather.18.cloned.1.call-update) | async-done | bytes 6291472 | tf_op jit(solution)/shard_map/all_gather | solution.py:83
  539.9 20.7 %fusion.75 = (bf16[1024]{0:T(1024)(128)(2,1)}, bf16[3072,1024]{1,0:T(8,128)(2,1)S(1)}) fusion(f32[3072,1024]{1,0:T(8,128)} %fusion.85, f32[1024]{0:T(1024)S(1)} %reshape.298, bf16[3072,1024]{1,0:T(8,128)(2,1)} %all-gather.18.cloned.1.call-done, bf16[1024,1024]{1,0:T(8,128)(2,1)} %all-gather.16.cloned.1.call-done), kind=kOutput, calls=%fused_computation.131 | convolution fusion | flops 6511655936 | bytes 27269120 | tf_op jit(solution)/shard_map/dot_general | solution.py:74
  572.6 99.7 %reduce-scatter.19.cloned.1.call-done = f32[768,1024]{1,0:T(8,128)} async-done(((f32[3072,1024]{1,0:T(8,128)}), f32[768,1024]{1,0:T(8,128)}) %reduce-scatter.19.cloned.1.call-update) | async-done | bytes 3145744 | tf_op jit(solution)/shard_map/reduce_scatter | solution.py:100
  679.9 12.8 %convolution_convert_fusion.1 = bf16[1024,1024]{1,0:T(8,128)(2,1)} fusion(bf16[3072,1024]{1,0:T(8,128)(2,1)} %all-gather.18.cloned.1.call-done, f32[3072,1024]{1,0:T(8,128)} %fusion.85, f32[1024]{0:T(1024)S(1)} %reshape.298), kind=kOutput, calls=%fused_computation.106 | convolution fusion | flops 6474956800 | bytes 20975616 | tf_op jit(solution)/shard_map/dot_general | solution.py:71
  692.8 11.7 convolution_convert_fusion.2
  704.6 21.8 %all-gather.20.cloned.1.call-done = bf16[3072,1024]{1,0:T(8,128)(2,1)} async-done(((bf16[768,1024]{1,0:T(8,128)(2,1)}), bf16[3072,1024]{1,0:T(8,128)(2,1)}) %all-gather.20.cloned.1.call-update) | async-done | bytes 6291472 | tf_op jit(solution)/shard_map/all_gather | solution.py:83
  740.3 113.8 %while.56 = (s32[]{:T(128)}, bf16[3,1024,768]{1,2,0:T(8,128)(2,1)}, bf16[3,1024,4,64]{1,3,2,0:T(8,128)(2,1)}, bf16[3,1024,4,64]{1,3,2,0:T(8,128)(2,1)}, f32[3,2,...) while((s32[]{:T(128)}, bf16[3,1024,768]{1,2,0:T(8,128)(2,1)}, ...), condition=%wide.region_19.20_spmd.clone, body=%wide.region_15.19_spmd.clone.sunk | while | flops 1380841984 | bytes 106000944 | solution.py:273
  747.7 27.1 %while.58 = (s32[]{:T(128)}, f32[1024,4,64]{0,2,1:T(8,128)S(1)}, f32[1024,4,64]{0,2,1:T(8,128)}, bf16[2,512,4,64]{1,3,2,0:T(8,128)(2,1)}, bf16[2,512,4,64]{1,3,2...) while((s32[]{:T(128)}, f32[1024,4,64]{0,2,1:T(8,128)S(1)}, ...), condition=%wide.region_18.18_spmd.clone, body=%wide.region_16.17_spmd.clone.sunk | while | flops 1375599104 | bytes 84996384 | solution.py:259
  785.6 27.1 %while.58 = (s32[]{:T(128)}, f32[1024,4,64]{0,2,1:T(8,128)S(1)}, f32[1024,4,64]{0,2,1:T(8,128)}, bf16[2,512,4,64]{1,3,2,0:T(8,128)(2,1)}, bf16[2,512,4,64]{1,3,2...) while((s32[]{:T(128)}, f32[1024,4,64]{0,2,1:T(8,128)S(1)}, ...), condition=%wide.region_18.18_spmd.clone, body=%wide.region_16.17_spmd.clone.sunk | while | flops 1375599104 | bytes 84996384 | solution.py:259
  823.4 27.1 %while.58 = (s32[]{:T(128)}, f32[1024,4,64]{0,2,1:T(8,128)S(1)}, f32[1024,4,64]{0,2,1:T(8,128)}, bf16[2,512,4,64]{1,3,2,0:T(8,128)(2,1)}, bf16[2,512,4,64]{1,3,2...) while((s32[]{:T(128)}, f32[1024,4,64]{0,2,1:T(8,128)S(1)}, ...), condition=%wide.region_18.18_spmd.clone, body=%wide.region_16.17_spmd.clone.sunk | while | flops 1375599104 | bytes 84996384 | solution.py:259
  895.3 36.1 %reduce-scatter.23.cloned.1.call-done = bf16[256,3,256]{2,0,1:T(8,128)(2,1)} async-done(((bf16[1024,3,256]{2,0,1:T(8,128)(2,1)}), bf16[256,3,256]{2,0,1:T(8,128)(2,1)}) %reduce-scatter.23.cloned.1.call-update) | async-done | bytes 393232 | tf_op jit(solution)/shard_map/reduce_scatter | solution.py:284
  931.5 10.4 fusion.87
  943.4 14.1 %fusion.73 = f32[3072,1024]{1,0:T(8,128)} fusion(bf16[1024,1024]{1,0:T(8,128)(2,1)S(1)} %copy-done.45, f32[3072,1024]{1,0:T(8,128)} %fusion.85, f32[1024]{0:T(1024)S(1)} %copy-done.42), kind=kOutput, calls=%fused_computation.129 | convolution fusion | flops 6473908224 | bytes 27267072 | tf_op jit(solution)/shard_map/dot_general | solution.py:61
  959.4 12.8 %reduce-scatter.31.cloned.1.call-done = bf16[16,8]{1,0:T(8,128)(2,1)} async-done(((bf16[64,8]{1,0:T(8,128)(2,1)}), bf16[16,8]{1,0:T(8,128)(2,1)}) %reduce-scatter.31.cloned.1.call-update) | async-done | bytes 272
  973.1 51.2 %all-reduce.18.cloned.1.call-done = (bf16[256,3,256]{2,0,1:T(8,128)(2,1)}, bf16[256,256]{1,0:T(8,128)(2,1)}, bf16[256,1024]{1,0:T(8,128)(2,1)}, bf16[1024,256]{1,0:T(8,128)(2,1)}) async-done(((bf16[256,3,256]{2,0,1:T(8,128)(2,1)}, bf16[256,256]{1,0:T(8,128)(2,1)}, bf16[256,1024]{1,0:T(8,128)(2,1)}, bf16[1024,256]{1,0:T(8,128)(2,1)}), (bf16[256,3,256]{2,0,1:T(8,128)(2,1)}, bf16[256,256]{1,0:T(8,128)(2,1)}, ...) | async-done | bytes 1572880 | tf_op jit(solution)/shard_map/psum | solution.py:315
  1031.1 95.3 %reduce-scatter.21.cloned.1.call-done = f32[768,1024]{1,0:T(8,128)} async-done(((f32[3072,1024]{1,0:T(8,128)}), f32[768,1024]{1,0:T(8,128)}) %reduce-scatter.21.cloned.1.call-update) | async-done | bytes 3145744 | tf_op jit(solution)/shard_map/reduce_scatter | solution.py:100
  1134.4 61.2 %all-reduce.12 = (f32[1024]{0:T(1024)S(1)}, bf16[1024]{0:T(1024)(128)(2,1)S(1)}, bf16[1024]{0:T(1024)(128)(2,1)S(1)}, bf16[1024]{0:T(1024)(128)(2,1)S(1)}, bf16[...) all-reduce(f32[1024]{0:T(1024)S(1)} %dynamic-update-slice.5, ...), channel_id=1, replica_groups=mesh['replica'=2,'fsdp'=4,'tensor'=4] {'fsdp','tensor'}, use_global_device_ids=true, to_apply=%add.5 | all-reduce | flops 7168 | bytes 45056
  1205.3 23.9 %reduce-scatter.17.cloned.1.call-done = f32[768,1024]{1,0:T(8,128)} async-done(((f32[3072,1024]{1,0:T(8,128)}), f32[768,1024]{1,0:T(8,128)}) %reduce-scatter.17.cloned.1.call-update) | async-done | bytes 3145744 | tf_op jit(solution)/shard_map/reduce_scatter | solution.py:60
  (495 shorter events, 362.4 us)
Async XLA Ops:
  7.2 74.4 %copy-start.2 = (bf16[768,1024]{1,0:T(8,128)(2,1)S(1)}, bf16[768,1024]{1,0:T(8,128)(2,1)}, u32[]{:S(2)}) copy-start(bf16[768,1024]{1,0:T(8,128)(2,1)} %param.22) | copy-start | bytes 4718596
  7.2 107.3 %all-gather.10.cloned.1.call-start = ((), (), s32[]{:S(2)}) async-start(), calls=%async_computation.11 | async-start | bytes 1966080 | tf_op jit(solution)/shard_map/all_gather | solution.py:143
  9.3 119.6 %all-gather.8.cloned.1.call-start = ((), (), s32[]{:S(2)}) async-start(), calls=%async_computation.10 | async-start | bytes 7864320 | tf_op jit(solution)/shard_map/all_gather | solution.py:56
  81.6 17.3 %copy-start.25 = (bf16[256,256]{1,0:T(8,128)(2,1)S(1)}, bf16[256,256]{1,0:T(8,128)(2,1)}, u32[]{:S(2)}) copy-start(bf16[256,256]{1,0:T(8,128)(2,1)} %param.27) | copy-start | bytes 393220
  85.1 266.4 %reduce-scatter.15.cloned.1.call-start = ((), (), s32[]{:S(2)}) async-start(), calls=%async_computation.12 | async-start | bytes 15728640 | tf_op jit(solution)/shard_map/reduce_scatter | solution.py:60
  251.8 99.7 %copy-start.39 = (f32[1024]{0:T(1024)S(1)}, f32[1024]{0:T(1024)}, u32[]{:S(2)}) copy-start(f32[1024]{0:T(1024)} %get-tuple-element.506) | copy-start | bytes 12292
  251.9 147.0 %all-gather.14.cloned.1.call-start = ((), (), s32[]{:S(2)}) async-start(), calls=%async_computation.14 | async-start | bytes 2621440 | tf_op jit(solution)/shard_map/all_gather | solution.py:146
  252.4 193.6 %all-gather.12.cloned.1.call-start = ((), (), s32[]{:S(2)}) async-start(), calls=%async_computation.13 | async-start | bytes 7864320 | tf_op jit(solution)/shard_map/all_gather | solution.py:56
  354.4 321.6 %copy-start = (f32[768,1024]{1,0:T(8,128)}, f32[768,1024]{1,0:T(8,128)S(1)}, u32[]{:S(2)}) copy-start(f32[768,1024]{1,0:T(8,128)S(1)} %get-tuple-element.528) | copy-start | bytes 9437188
  356.9 136.8 %all-gather.16.cloned.1.call-start = ((), (), s32[]{:S(2)}) async-start(), calls=%async_computation.15 | async-start | bytes 2621440 | tf_op jit(solution)/shard_map/all_gather | solution.py:148
  357.5 182.4 %all-gather.18.cloned.1.call-start = ((), (), s32[]{:S(2)}) async-start(), calls=%async_computation.17 | async-start | bytes 7864320 | tf_op jit(solution)/shard_map/all_gather | solution.py:83
  358.3 314.1 %reduce-scatter.19.cloned.1.call-start = ((), (), s32[]{:S(2)}) async-start(), calls=%async_computation.18 | async-start | bytes 15728640 | tf_op jit(solution)/shard_map/reduce_scatter | solution.py:100
  372.1 307.8 %copy-start.41 = (f32[1024]{0:T(1024)}, f32[1024]{0:T(1024)S(1)}, u32[]{:S(2)}) copy-start(f32[1024]{0:T(1024)S(1)} %reshape.298) | copy-start | bytes 12292
  539.9 23.3 %copy-start.46 = (bf16[1024,1024]{1,0:T(8,128)(2,1)S(1)}, bf16[1024,1024]{1,0:T(8,128)(2,1)}, u32[]{:S(2)}) copy-start(bf16[1024,1024]{1,0:T(8,128)(2,1)} %all-gather.14.cloned.1.call-done) | copy-start | bytes 6291460
  572.6 153.8 %all-gather.20.cloned.1.call-start = ((), (), s32[]{:S(2)}) async-start(), calls=%async_computation.19 | async-start | bytes 7864320 | tf_op jit(solution)/shard_map/all_gather | solution.py:83
  679.9 208.2 %reduce-scatter.29.cloned.1.call-start = ((), (), s32[]{:S(2)}) async-start(), calls=%async_computation.24 | async-start | bytes 2621440 | tf_op jit(solution)/shard_map/reduce_scatter | solution.py:302
  692.7 195.4 %reduce-scatter.27.cloned.1.call-start = ((), (), s32[]{:S(2)}) async-start(), calls=%async_computation.23 | async-start | bytes 2621440 | tf_op jit(solution)/shard_map/reduce_scatter | solution.py:293
  692.8 33.6 %copy-start.21 = (bf16[256,1024]{1,0:T(8,128)(2,1)S(1)}, bf16[256,1024]{1,0:T(8,128)(2,1)}, u32[]{:S(2)}) copy-start(bf16[256,1024]{1,0:T(8,128)(2,1)} %all_gather.59) | copy-start | bytes 1572868
  704.6 190.8 %reduce-scatter.25.cloned.1.call-start = ((), (), s32[]{:S(2)}) async-start(), calls=%async_computation.22 | async-start | bytes 655360 | tf_op jit(solution)/shard_map/reduce_scatter | solution.py:290
  873.3 58.1 %reduce-scatter.23.cloned.1.call-start = ((), (), s32[]{:S(2)}) async-start(), calls=%async_computation.21 | async-start | bytes 1966080 | tf_op jit(solution)/shard_map/reduce_scatter | solution.py:284
  882.9 75.7 %reduce-scatter.33.cloned.1.call-start = ((), (), s32[]{:S(2)}) async-start(), calls=%async_computation.26 | async-start | bytes 20480
  883.8 47.7 %copy-start.47 = (bf16[1024,3,256]{0,2,1:T(8,128)(2,1)S(1)}, bf16[1024,3,256]{0,2,1:T(8,128)(2,1)}, u32[]{:S(2)}) copy-start(bf16[1024,3,256]{0,2,1:T(8,128)(2,1)} %all-gather.10.cloned.1.call-done) | copy-start | bytes 4718596
  883.8 88.4 %reduce-scatter.31.cloned.1.call-start = ((), (), s32[]{:S(2)}) async-start(), calls=%async_computation.25 | async-start | bytes 20480
  888.0 136.2 %all-reduce.18.cloned.1.call-start = ((), (), s32[]{:S(2)}) async-start(), calls=%async_computation.27 | async-start | bytes 3145728 | tf_op jit(solution)/shard_map/psum | solution.py:315
  931.4 194.9 %reduce-scatter.21.cloned.1.call-start = ((), (), s32[]{:S(2)}) async-start(), calls=%async_computation.20 | async-start | bytes 15728640 | tf_op jit(solution)/shard_map/reduce_scatter | solution.py:100
  941.8 287.4 %reduce-scatter.17.cloned.1.call-start = ((), (), s32[]{:S(2)}) async-start(), calls=%async_computation.16 | async-start | bytes 15728640 | tf_op jit(solution)/shard_map/reduce_scatter | solution.py:60
  957.6 168.8 %copy-start.3 = (bf16[768,1024]{1,0:T(8,128)(2,1)S(1)}, bf16[768,1024]{1,0:T(8,128)(2,1)}, u32[]{:S(2)}) copy-start(bf16[768,1024]{1,0:T(8,128)(2,1)} %param.22) | copy-start | bytes 4718596
  957.6 168.8 %copy-start.24 = (f32[768]{0:T(1024)S(1)}, f32[768]{0:T(1024)}, u32[]{:S(2)}) copy-start(f32[768]{0:T(1024)} %copy-done.23) | copy-start | bytes 9220
  957.6 168.7 %copy-start.27 = (f32[1024]{0:T(1024)S(1)}, f32[1024]{0:T(1024)}, u32[]{:S(2)}) copy-start(f32[1024]{0:T(1024)} %copy-done.26) | copy-start | bytes 12292
  1030.0 99.2 %copy-start.34 = (f32[768]{0:T(1024)S(1)}, f32[768]{0:T(1024)}, u32[]{:S(2)}) copy-start(f32[768]{0:T(1024)} %copy-done.33) | copy-start | bytes 9220
  1030.0 99.2 %copy-start.29 = (f32[768]{0:T(1024)S(1)}, f32[768]{0:T(1024)}, u32[]{:S(2)}) copy-start(f32[768]{0:T(1024)} %copy-done.28) | copy-start | bytes 9220
  1131.6 97.6 %copy-start.1 = (f32[768,1024]{1,0:T(8,128)S(1)}, f32[768,1024]{1,0:T(8,128)}, u32[]{:S(2)}) copy-start(f32[768,1024]{1,0:T(8,128)} %copy-done) | copy-start | bytes 9437188
  (73 other events, 173.5 us)
Sparse Core Ops, SparseCore 0:
  10.1 40.7 all-gather.9
  85.2 43.6 all-gather.7
  252.0 99.5 reduce-scatter.14
  353.0 45.8 all-gather.13
  400.8 45.1 all-gather.11
  447.5 46.2 all-gather.15
  495.3 44.5 all-gather.17
  572.7 99.6 reduce-scatter.18
  680.0 46.3 all-gather.19
  728.5 43.6 reduce-scatter.28
  774.5 42.8 reduce-scatter.26
  873.4 21.8 reduce-scatter.24
  897.6 33.7 reduce-scatter.22
  934.0 18.0 reduce-scatter.32
  954.8 17.3 reduce-scatter.30
  974.5 49.6 all-reduce.17
  1026.7 99.5 reduce-scatter.20
  1128.8 100.3 reduce-scatter.16
where the time goes:
time: 1250 us; the launch traced here: 1240 us
  waiting for transfers between devices  619 us (50%)
  matrix products  214 us (17%)
  blocking collectives  173 us (14%)
  local copies, waits for them, and re-layouts  128 us (10%)
  other arithmetic  87.3 us (7%)
  between operations  16.4 us (1%)
    reduce_scatter x2, waiting for transfers between devices, back_normed(): lax.psum_scatter(lax.dot_general(grad, weight, (((1,), (1,)), ((), ())),...  195 us
    unnamed x2, blocking collectives  125 us
    reduce_scatter x2, waiting for transfers between devices, gather_sum(): lax.psum_scatter(jnp.dot(left, right, preferred_element_type=jnp.float32)...  123 us
    all_gather x2, waiting for transfers between devices, back_rows(): lax.all_gather(local_grad, 'tensor', axis=0, tiled=True)  67.9 us
    all_gather x2, waiting for transfers between devices, spread_rows(): lax.all_gather(local, 'tensor', axis=0, tiled=True)  61.6 us
    psum x1, waiting for transfers between devices, on_device(): lax.psum(fsdp_sums[0].astype(jnp.bfloat16), 'replica').astype(jnp.float32)  51.2 us
    unnamed x118, local copies, waits for them, and re-layouts  37.2 us
    reduce_scatter x1, waiting for transfers between devices, on_device(): lax.psum_scatter(grad_joined.astype(jnp.bfloat16), 'fsdp', scatter_dimens...  36.1 us
  transfers between devices with their start and end apart: 18, of which 14 were waited for; matrix products, arithmetic and copies ran while one was open for 21% of the time, Pallas kernels for 0%

commit v1 on v0

v1 whole, which is shorter than its diff:
```python
import jax
import jax.numpy as jnp
from jax import lax
from jax.experimental import pallas as pl
from jax.experimental.pallas import tpu as pltpu
from jax.sharding import PartitionSpec as P

HD = 64
LEN = 1024


EPS = 1e-05
NEG = -1e30
BLOCK = 256
BF = jnp.bfloat16
F32 = jnp.float32


def dot(left, right, dims):
    return lax.dot_general(left, right, (dims, ((), ())), preferred_element_type=F32)


def mm(left, right):
    return dot(left, right, ((1,), (0,)))


def mm_t(left, right):
    return dot(left, right, ((1,), (1,)))


def t_mm(left, right):
    return dot(left, right, ((0,), (0,)))


def layer_norm(values, gain, bias):
    center = values - jnp.mean(values, -1, keepdims=True)
    spread = jnp.mean(center * center, -1, keepdims=True)
    return center * lax.rsqrt(spread + EPS) * gain + bias


def gelu_tanh(values):
    return jax.nn.gelu(values, approximate=True)


def swap(value, bit):
    size = lax.axis_size("tensor")
    return lax.ppermute(value, "tensor", [(i, i ^ bit) for i in range(size)])


def after(value, *others):
    return lax.optimization_barrier((value,) + others)[0]


def chunk_count():
    size = lax.axis_size("tensor")
    return 4 if size == 4 else 1


def gather_rows(local):
    if chunk_count() == 1:
        return [lax.all_gather(local, "tensor", axis=0, tiled=True)]
    sib = swap(local, 1)
    far = swap(local, 2)
    return [local, sib, far, swap(far, 1)]


def sum_rows(part):
    if chunk_count() == 1:
        return lax.psum_scatter(part(0), "tensor", scatter_dimension=0, tiled=True)
    side = swap(part(3).astype(BF), 1)
    cross = swap((part(2) + side.astype(F32)).astype(BF), 2)
    near = swap(part(1).astype(BF), 1)
    return part(0) + near.astype(F32) + cross.astype(F32)


def take_rows(full, k):
    if chunk_count() == 1:
        return full
    rows = full.shape[0] // 4
    return lax.dynamic_slice_in_dim(full, (lax.axis_index("tensor") ^ k) * rows, rows, 0)


def in_order(pieces):
    if len(pieces) == 1:
        return pieces[0]
    rows = pieces[0].shape[0]
    me = lax.axis_index("tensor")
    full = jnp.zeros((4 * rows, pieces[0].shape[1]), pieces[0].dtype)
    for k, piece in enumerate(pieces):
        full = lax.dynamic_update_slice_in_dim(full, piece, (me ^ k) * rows, 0)
    return full


def joined_rows(pieces):
    return pieces[0] if len(pieces) == 1 else jnp.concatenate(pieces, 0)


def replica_sum(value):
    size = lax.axis_size("replica")
    if size == 2:
        return value.astype(F32) + lax.ppermute(value, "replica", [(0, 1), (1, 0)]).astype(F32)
    return lax.psum(value, "replica").astype(F32)


def scores_t(qkv_ref, width, head, block):
    stop = (block + 1) * BLOCK
    low = head * HD
    query = qkv_ref[block * BLOCK : stop, low : low + HD]
    keys = qkv_ref[0:stop, width + low : width + low + HD]
    scores = mm_t(keys, query * jnp.asarray(HD ** (-0.5), BF))
    shape = (BLOCK, BLOCK)
    keep = lax.broadcasted_iota(jnp.int32, shape, 0) <= lax.broadcasted_iota(jnp.int32, shape, 1)
    edge = jnp.where(keep, scores[stop - BLOCK :], NEG)
    scores = edge if block == 0 else jnp.concatenate([scores[: stop - BLOCK], edge], 0)
    expo = jnp.exp(scores - jnp.max(scores, 0, keepdims=True))
    return query, keys, expo, 1.0 / jnp.sum(expo, 0, keepdims=True)


def attend_kernel(qkv_ref, out_ref):
    width = out_ref.shape[1]
    for pair in range(width // (2 * HD)):
        for block in range(LEN // BLOCK):
            stop = (block + 1) * BLOCK
            halves = []
            for head in (2 * pair, 2 * pair + 1):
                _, _, expo, inverse = scores_t(qkv_ref, width, head, block)
                low = 2 * width + head * HD
                values = qkv_ref[0:stop, low : low + HD]
                halves.append(t_mm(values, expo.astype(BF)) * inverse)
            out_ref[block * BLOCK : stop, pair * 2 * HD : (pair + 1) * 2 * HD] = (
                jnp.concatenate(halves, 0).T.astype(BF)
            )


def attend_back_kernel(qkv_ref, grad_ref, out_ref, keys_sum, values_sum):
    width = grad_ref.shape[1]
    scale = HD ** (-0.5)
    for pair in range(width // (2 * HD)):
        for block in reversed(range(LEN // BLOCK)):
            stop = (block + 1) * BLOCK
            halves = []
            for side in (0, 1):
                head = 2 * pair + side
                query, keys, expo, inverse = scores_t(qkv_ref, width, head, block)
                low = head * HD
                values = qkv_ref[0:stop, 2 * width + low : 2 * width + low + HD]
                grad = grad_ref[block * BLOCK : stop, low : low + HD]
                probs = expo * inverse
                grad_values = mm(probs.astype(BF), grad)
                grad_probs = mm_t(values, grad)
                weighted = probs * grad_probs
                total = jnp.sum(weighted, 0, keepdims=True)
                grad_scores = (weighted - probs * total).astype(BF)
                grad_keys = mm(grad_scores, query)
                lanes = slice(side * HD, (side + 1) * HD)
                if stop == LEN:
                    values_sum[:, lanes] = grad_values
                    keys_sum[:, lanes] = grad_keys
                else:
                    values_sum[0:stop, lanes] += grad_values
                    keys_sum[0:stop, lanes] += grad_keys
                halves.append(t_mm(keys, grad_scores))
            low = pair * 2 * HD
            out_ref[block * BLOCK : stop, low : low + 2 * HD] = (
                jnp.concatenate(halves, 0).T * scale
            ).astype(BF)
        out_ref[:, width + low : width + low + 2 * HD] = (keys_sum[...] * scale).astype(BF)
        out_ref[:, 2 * width + low : 2 * width + low + 2 * HD] = values_sum[...].astype(BF)


def rows_spec(width):
    return pl.BlockSpec((LEN, width), lambda i: (i, 0))


def attend(qkv):
    rows, width = qkv.shape[0], qkv.shape[1] // 3
    return pl.pallas_call(
        attend_kernel,
        grid=(rows // LEN,),
        in_specs=[rows_spec(3 * width)],
        out_specs=rows_spec(width),
        out_shape=jax.ShapeDtypeStruct((rows, width), BF),
        cost_estimate=pl.CostEstimate(
            flops=24_000_000_000, bytes_accessed=8 * rows * width, transcendentals=rows * width * 4
        ),
        compiler_params=pltpu.CompilerParams(vmem_limit_bytes=48 * 1024 * 1024),
        name="attend",
    )(qkv)


def attend_back(qkv, grad):
    rows, width = grad.shape
    return pl.pallas_call(
        attend_back_kernel,
        grid=(rows // LEN,),
        in_specs=[rows_spec(3 * width), rows_spec(width)],
        out_specs=rows_spec(3 * width),
        out_shape=jax.ShapeDtypeStruct((rows, 3 * width), BF),
        scratch_shapes=[pltpu.VMEM((LEN, 2 * HD), F32), pltpu.VMEM((LEN, 2 * HD), F32)],
        cost_estimate=pl.CostEstimate(
            flops=48_000_000_000, bytes_accessed=14 * rows * width, transcendentals=rows * width * 4
        ),
        compiler_params=pltpu.CompilerParams(vmem_limit_bytes=48 * 1024 * 1024),
        name="attend_back",
    )(qkv, grad)


def pack(flat):
    size = flat.shape[-1]
    full = -(-size // 1024) * 1024
    flat = jnp.pad(flat, [(0, 0)] * (flat.ndim - 1) + [(0, full - size)])
    return flat.reshape(flat.shape[:-1] + (full // 128, 128))


def on_device(
    tokens,
    ln1_gain,
    ln1_bias,
    qkv_weight,
    qv_bias,
    out_weight,
    out_bias,
    ln2_gain,
    ln2_bias,
    fc_weight,
    fc_bias,
    proj_weight,
    proj_bias,
    out_grad,
):
    both = ("fsdp", "tensor")
    n_fsdp, n_tensor = lax.axis_size("fsdp"), lax.axis_size("tensor")
    me = lax.axis_index("tensor")
    part = ln1_gain.shape[0]
    width = out_weight.shape[0]
    heads = width // HD
    hidden = fc_weight.shape[1]
    model = tokens.shape[1]
    vectors = jnp.concatenate(
        [
            ln1_gain,
            ln1_bias,
            ln2_gain,
            ln2_bias,
            out_bias,
            proj_bias,
            qv_bias.astype(F32).reshape(-1),
            fc_bias.astype(F32).reshape(-1),
        ]
    )
    bundle = lax.all_gather(pack(vectors), both, axis=0, tiled=False)
    bundle = bundle.reshape(n_fsdp * n_tensor, -1)
    gain_one, bias_one, gain_two, bias_two, bias_out, bias_proj = (
        bundle[:, i * part : (i + 1) * part].reshape(-1) for i in range(6)
    )
    mine = lax.dynamic_index_in_dim(bundle.reshape(n_fsdp, n_tensor, -1), me, 1, keepdims=False)
    low, high = 6 * part, 6 * part + qv_bias.size
    qv_full = (
        mine[:, low:high].reshape((n_fsdp,) + qv_bias.shape).transpose(1, 2, 0, 3).reshape(2, width)
    )
    fcb_full = (
        mine[:, high : high + fc_bias.size]
        .reshape((n_fsdp,) + fc_bias.shape)
        .transpose(1, 0, 2)
        .reshape(hidden)
    )
    bias_row = jnp.concatenate([qv_full[0], jnp.zeros((width,), F32), qv_full[1]])
    joined = lax.all_gather(
        qkv_weight.reshape(qkv_weight.shape[0], 3 * width), "fsdp", axis=0, tiled=True
    )
    out_full = lax.all_gather(out_weight, "fsdp", axis=1, tiled=True)
    fc_full = lax.all_gather(fc_weight, "fsdp", axis=0, tiled=True)
    proj_full = lax.all_gather(proj_weight, "fsdp", axis=1, tiled=True)

    inputs = tokens.astype(F32)
    normed_one = gather_rows(layer_norm(inputs, gain_one, bias_one).astype(BF))
    qkv = in_order([(mm(piece, joined) + bias_row).astype(BF) for piece in normed_one])
    attended = attend(qkv)
    att = [take_rows(attended, k) for k in range(chunk_count())]
    grads = gather_rows(after(out_grad, qkv))
    middle = inputs + (sum_rows(lambda k: mm(att[k], out_full)) + bias_out)
    normed_two = gather_rows(layer_norm(middle, gain_two, bias_two).astype(BF))
    before = [mm(piece, fc_full) + fcb_full for piece in normed_two]
    act = [gelu_tanh(piece).astype(BF) for piece in before]

    grad_pre = []
    for piece, grad in zip(before, grads):
        pull = jax.vjp(gelu_tanh, piece)[1]
        grad_pre.append(pull(mm_t(grad, proj_full))[0].astype(BF))
    grad_normed_two = sum_rows(lambda k: mm_t(grad_pre[k], fc_full))
    grad_pre_all = joined_rows(grad_pre)
    grad_proj = t_mm(joined_rows(act), joined_rows(grads)).astype(BF)
    grad_fc = t_mm(joined_rows(normed_two), grad_pre_all).astype(BF)
    grad_fc_bias = jnp.sum(grad_pre_all, 0, dtype=F32)
    grad_proj_bias = jnp.sum(out_grad, 0, dtype=F32)
    norm_pull_two = jax.vjp(layer_norm, middle, gain_two, bias_two)[1]
    grad_middle_part, grad_gain_two, grad_bias_two = norm_pull_two(grad_normed_two)
    grad_middle = out_grad.astype(F32) + grad_middle_part
    grad_branch = grad_middle.astype(BF)
    grad_out_bias = jnp.sum(grad_branch, 0, dtype=F32)
    branches = gather_rows(grad_branch)
    grad_attended = in_order([mm_t(piece, out_full).astype(BF) for piece in branches])

    late = lax.optimization_barrier((grad_attended, *act))
    grad_attended, act = late[0], late[1:]
    output = middle + sum_rows(lambda k: mm(act[k], proj_full)) + bias_proj
    grad_qkv = attend_back(qkv, grad_attended)
    grad_out = t_mm(joined_rows(att), joined_rows(branches)).astype(BF)
    pieces = [take_rows(grad_qkv, k) for k in range(chunk_count())]
    grad_normed_one = sum_rows(lambda k: mm_t(pieces[k], joined))
    pieces_all = joined_rows(pieces)
    grad_joined = t_mm(joined_rows(normed_one), pieces_all).astype(BF)
    qkv_sums = jnp.sum(pieces_all, 0, dtype=F32)
    norm_pull_one = jax.vjp(layer_norm, inputs, gain_one, bias_one)[1]
    grad_input_part, grad_gain_one, grad_bias_one = norm_pull_one(grad_normed_one)
    input_grad = grad_middle + grad_input_part

    def scatter(value, dim):
        return replica_sum(
            lax.psum_scatter(value, "fsdp", scatter_dimension=dim, tiled=True).astype(BF)
        )

    total_proj = scatter(grad_proj, 1)
    total_fc = scatter(grad_fc, 0)
    total_out = scatter(grad_out, 1)
    total_joined = scatter(grad_joined, 0)

    wide = jnp.stack(
        [grad_gain_one, grad_bias_one, grad_gain_two, grad_bias_two, grad_out_bias, grad_proj_bias]
    )
    wide = wide.reshape(6, n_fsdp * n_tensor, part).transpose(1, 0, 2).reshape(-1, 6 * part)
    grad_qv = jnp.stack([qkv_sums[:width], qkv_sums[2 * width :]])
    grad_qv = grad_qv.reshape(2, heads, n_fsdp, -1).transpose(2, 0, 1, 3).reshape(n_fsdp, -1)
    grad_fcb = grad_fc_bias.reshape(fc_bias.shape[0], n_fsdp, -1).transpose(1, 0, 2)
    own = jnp.concatenate([grad_qv, grad_fcb.reshape(n_fsdp, -1)], -1)
    is_me = (jnp.arange(n_tensor, dtype=jnp.int32) == me)[None, :, None]
    own = jnp.where(is_me, own[:, None, :], 0.0).reshape(n_fsdp * n_tensor, -1)
    sums = lax.psum_scatter(
        pack(jnp.concatenate([wide, own], -1)), both, scatter_dimension=0, tiled=False
    )
    sums = replica_sum(sums).reshape(-1)
    vec = [sums[i * part : (i + 1) * part] for i in range(6)]
    total_qv = sums[low:high].reshape(qv_bias.shape)
    total_fcb = sums[high : high + fc_bias.size].reshape(fc_bias.shape)
    return (
        output,
        input_grad,
        vec[0],
        vec[1],
        total_joined.reshape(qkv_weight.shape),
        total_qv,
        total_out,
        vec[4],
        vec[2],
        vec[3],
        total_fc,
        total_fcb,
        total_proj,
        vec[5],
    )


def solution(mesh):
    placed = (
        P(("replica", "fsdp", "tensor"), None),
        P(("fsdp", "tensor")),
        P(("fsdp", "tensor")),
        P("fsdp", None, "tensor"),
        P(None, "tensor", "fsdp"),
        P("tensor", "fsdp"),
        P(("fsdp", "tensor")),
        P(("fsdp", "tensor")),
        P(("fsdp", "tensor")),
        P("fsdp", "tensor"),
        P("tensor", "fsdp"),
        P("tensor", "fsdp"),
        P(("fsdp", "tensor")),
        P(("replica", "fsdp", "tensor"), None),
    )
    return jax.shard_map(
        on_device,
        mesh=mesh,
        in_specs=placed,
        out_specs=(
            P(("replica", "fsdp", "tensor"), None),
            P(("replica", "fsdp", "tensor"), None),
            P(("fsdp", "tensor")),
            P(("fsdp", "tensor")),
            P("fsdp", None, "tensor"),
            P(None, "tensor", "fsdp"),
            P("tensor", "fsdp"),
            P(("fsdp", "tensor")),
            P(("fsdp", "tensor")),
            P(("fsdp", "tensor")),
            P("fsdp", "tensor"),
            P("tensor", "fsdp"),
            P("tensor", "fsdp"),
            P(("fsdp", "tensor")),
        ),
        check_vma=False,
    )
```

time: 1250 us -> 661 us (0.53)
  waiting for transfers between devices: 619 us -> 273 us
  blocking collectives: 173 us -> 45.5 us
  local copies, waits for them, and re-layouts: 128 us -> 36.5 us
  Pallas kernels: 0 us -> 68.2 us
  matrix products: 214 us -> 151 us
  other arithmetic: 87.3 us -> 43.6 us
  starting transfers between devices: 0.73 us -> 20 us
    reduce_scatter x8 -> x4, waiting for transfers between devices: 361 us -> 0.01 us  [scatter(): lax.psum_scatter(value, 'fsdp', scatter_dimension=dim, tiled=True)]
    all_gather x7 -> x3, waiting for transfers between devices: 192 us -> 0.01 us  [the longest x1 0.01 us: on_device(): lax.all_gather(qkv_weight.reshape(qkv_weight.shape[0], 3 * width), 'fsdp'...]
    ppermute x0 -> x29, waiting for transfers between devices: none -> 190 us  [the longest x24 181 us: swap(): return lax.ppermute(value, 'tensor', [(i, i ^ bit) for i in range(size)])]
    unnamed x2 -> x0, blocking collectives: 125 us -> none
    unnamed x20 -> x9, waiting for transfers between devices: 14.8 us -> 83.6 us
    pallas_call x0 -> x2, Pallas kernels: none -> 68.2 us  [the longest x1 43.6 us: attend_back(): pl.pallas_call(attend_back_kernel, grid=(rows // LEN,), in_specs=[rows_sp...]
    dot_general x54 -> x36, matrix products: 214 us -> 151 us  [dot(): lax.dot_general(left, right, (dims, ((), ())), preferred_element_type=F32)]
    psum x1 -> x0, waiting for transfers between devices: 51.2 us -> none  [on_device(): lax.psum(fsdp_sums[0].astype(jnp.bfloat16), 'replica').astype(jnp.float32)]
  transfers between devices with their start and end apart: 18 -> 37, of which waited for: 14 -> 10; matrix products, arithmetic and copies ran while one was open for 21% -> 29% of each run, Pallas kernels for 0% -> 10%
where the time goes in v1:
time: 661 us; the launch traced here: 653 us
  waiting for transfers between devices  273 us (41%)
  matrix products  151 us (23%)
  Pallas kernels  68.2 us (10%)
  blocking collectives  45.5 us (7%)
  other arithmetic  43.6 us (7%)
  local copies, waits for them, and re-layouts  36.5 us (6%)
  starting transfers between devices  20 us (3%)
  between operations  15.5 us (2%)
    ppermute x24, waiting for transfers between devices, swap(): return lax.ppermute(value, 'tensor', [(i, i ^ bit) for i in range(size)])  181 us
    dot_general x36, matrix products, dot(): lax.dot_general(left, right, (dims, ((), ())), preferred_element_type=F32)  151 us
    unnamed x9, waiting for transfers between devices  83.6 us
    pallas_call x1, Pallas kernels, attend_back(): pl.pallas_call(attend_back_kernel, grid=(rows // LEN,), in_specs=[rows_sp...  43.6 us
    pallas_call x1, Pallas kernels, attend(): pl.pallas_call(attend_kernel, grid=(rows // LEN,), in_specs=[rows_spec(3...  24.6 us
    all_gather x1, blocking collectives, on_device(): bundle = lax.all_gather(pack(vectors), both, axis=0, tiled=False)  23.8 us
    all_gather x1, blocking collectives, on_device(): out_full = lax.all_gather(out_weight, 'fsdp', axis=1, tiled=True)  21.6 us
  transfers between devices with their start and end apart: 37, of which 10 were waited for; matrix products, arithmetic and copies ran while one was open for 29% of the time, Pallas kernels for 10%

profile of v1, /device:TPU:0, one launch (start us, length us, event | category | flops | bytes accessed | tf_op | source)
XLA Modules:
  0.0 653.3 jit_solution(10428699731758847327)
XLA Ops:
  11.7 23.8 %all_gather.15 = f32[16,8,128]{2,1,0:T(8,128)S(1)} all-gather(f32[1,8,128]{2,1,0:T(8,128)S(1)} %pad_bitcast_fusion), channel_id=1, replica_groups=mesh['replica'=2,'fsdp'=4,'tensor'=4] {'fsdp','tensor'}, dimensions={0}, use_global_device_ids=true | all-gather | bytes 69632 | tf_op jit(solution)/shard_map/all_gather | solution.py:251
  40.7 36.1 %collective-permute-done.1 = bf16[768,1024]{1,0:T(8,128)(2,1)} collective-permute-done((bf16[768,1024]{1,0:T(8,128)(2,1)S(1)}, bf16[768,1024]{1,0:T(8,128)(2,1)}, u32[]{:S(2)}, u32[]{:S(2)}) %collective-permute-start.1) | collective-permute-done | bytes 1572896 | tf_op jit(solution)/shard_map/ppermute | solution.py:47
  77.0 21.6 %all_gather.17 = bf16[256,1024]{1,0:T(8,128)(2,1)S(1)} all-gather(bf16[256,256]{1,0:T(8,128)(2,1)S(1)} %copy-done.31), channel_id=1, replica_groups=mesh['replica'=2,'fsdp'=4,'tensor'=4] {'fsdp'}, dimensions={1}, use_global_device_ids=true | all-gather | bytes 655360 | tf_op jit(solution)/shard_map/all_gather | solution.py:271
  112.4 24.6 %attend.1 = bf16[3072,256]{1,0:T(8,128)(2,1)S(1)} custom-call(bf16[3072,768]{1,0:T(8,128)(2,1)} %copy-done.11), custom_call_target="tpu_custom_call" | custom-call | flops 24000000000 | bytes 6291456 | tf_op jit(solution)/shard_map/attend/pallas_call | solution.py:177
  148.6 31.9 %collective-permute-done.5 = bf16[768,1024]{1,0:T(8,128)(2,1)} collective-permute-done((bf16[768,1024]{1,0:T(8,128)(2,1)}, bf16[768,1024]{1,0:T(8,128)(2,1)}, u32[]{:S(2)}, u32[]{:S(2)}) %collective-permute-start.5) | collective-permute-done | bytes 1572896 | tf_op jit(solution)/shard_map/ppermute | solution.py:47
  192.6 21.7 %collective-permute-done.9 = bf16[768,1024]{1,0:T(8,128)(2,1)} collective-permute-done((bf16[768,1024]{1,0:T(8,128)(2,1)}, bf16[768,1024]{1,0:T(8,128)(2,1)}, u32[]{:S(2)}, u32[]{:S(2)}) %collective-permute-start.9) | collective-permute-done | bytes 1572896 | tf_op jit(solution)/shard_map/ppermute | solution.py:47
  214.3 5.7 fusion.127
  219.9 5.0 fusion.132
  225.4 4.9 fusion.130
  230.3 16.8 %collective-permute-done.10 = bf16[768,1024]{1,0:T(8,128)(2,1)} collective-permute-done((bf16[768,1024]{1,0:T(8,128)(2,1)}, bf16[768,1024]{1,0:T(8,128)(2,1)}, u32[]{:S(2)}, u32[]{:S(2)}) %collective-permute-start.10) | collective-permute-done | bytes 1572896 | tf_op jit(solution)/shard_map/ppermute | solution.py:47
  247.1 4.0 fusion.128
  251.2 5.0 fusion.134
  262.9 14.9 %multiply_convert_fusion = (bf16[768,1024]{1,0:T(8,128)(2,1)}, bf16[768,1024]{1,0:T(8,128)(2,1)}, bf16[768,1024]{1,0:T(8,128)(2,1)}, bf16[768,1024]{1,0:T(8,128)...) fusion(f32[1024]{0:T(1024)S(1)} %copy-done.53, ...), kind=kOutput, calls=%fused_computation.104 | convolution fusion | flops 1682964480 | bytes 38277120 | tf_op jit(solution)/shard_map/dot_general | solution.py:20
  277.8 12.7 %fusion.79 = bf16[1024,1024]{1,0:T(8,128)(2,1)} fusion(bf16[768,1024]{1,0:T(8,128)(2,1)} %collective-permute-done.11, bf16[768,1024]{1,0:T(8,128)(2,1)} %collective-permute-done.9, bf16[768,1024]{1,0:T(8,128)(2,1)} %collective-permute-done.6, bf16[768,1024]{1,0:T(8,128)(2,1)} %param.27, bf16[768,1024]{1,0:T(8,128)(2,1)} %get-tuple-element.24, ...), kind=kOutput, calls=%fused_computation.119 | convolution fusion | flops 6493831168 | bytes 14680064 | tf_op jit(solution)/shard_map/dot_general | solution.py:20
  290.9 4.0 convolution_convert_fusion.4
  302.4 12.0 %fusion.84 = bf16[1024,1024]{1,0:T(8,128)(2,1)} fusion(bf16[768,1024]{1,0:T(8,128)(2,1)} %collective-permute-done.12, bf16[768,1024]{1,0:T(8,128)(2,1)} %collective-permute-done.10, bf16[768,1024]{1,0:T(8,128)(2,1)} %collective-permute-done.7, bf16[768,1024]{1,0:T(8,128)(2,1)} %add_convert_fusion.3, bf16[768,1024]{1,0:T(8,128)(2,1)S(1)} %copy-done.16, ...), kind=kOutput, calls=%fused_computation.120 | convolution fusion | flops 6493831168 | bytes 14680064 | tf_op jit(solution)/shard_map/dot_general | solution.py:20
  314.9 3.9 fusion.129
  318.8 19.9 %collective-permute-done.14 = bf16[768,1024]{1,0:T(8,128)(2,1)} collective-permute-done((bf16[768,1024]{1,0:T(8,128)(2,1)}, bf16[768,1024]{1,0:T(8,128)(2,1)}, u32[]{:S(2)}, u32[]{:S(2)}) %collective-permute-start.14) | collective-permute-done | bytes 1572896 | tf_op jit(solution)/shard_map/ppermute | solution.py:47
  338.7 4.1 multiply_reduce_fusion
  343.9 4.3 convert_reduce_fusion.4
  352.5 31.8 %collective-permute-done.16 = bf16[768,1024]{1,0:T(8,128)(2,1)} collective-permute-done((bf16[768,1024]{1,0:T(8,128)(2,1)}, bf16[768,1024]{1,0:T(8,128)(2,1)}, u32[]{:S(2)}, u32[]{:S(2)}) %collective-permute-start.16) | collective-permute-done | bytes 1572896 | tf_op jit(solution)/shard_map/ppermute | solution.py:47
  397.5 8.6 %collective-permute-done.27 = bf16[256,1024]{1,0:T(8,128)(2,1)S(1)} collective-permute-done((bf16[256,1024]{1,0:T(8,128)(2,1)}, bf16[256,1024]{1,0:T(8,128)(2,1)S(1)}, u32[]{:S(2)}, u32[]{:S(2)}) %collective-permute-start.27) | collective-permute-done | bytes 524320 | tf_op jit(solution)/shard_map/ppermute | solution.py:101
  411.4 4.6 fusion.101
  418.1 43.6 %attend_back.1 = bf16[3072,768]{1,0:T(8,128)(2,1)} custom-call(bf16[3072,768]{1,0:T(8,128)(2,1)} %copy-done.11, bf16[3072,256]{1,0:T(8,128)(2,1)S(1)} %fusion.106.grad_ref), custom_call_target="tpu_custom_call" | custom-call | flops 48000000000 | bytes 11010048 | tf_op jit(solution)/shard_map/attend_back/pallas_call | solution.py:193
  475.9 5.2 convolution_convert_fusion.2
  484.5 8.7 %fusion.87 = bf16[1024,768]{1,0:T(8,128)(2,1)} fusion(bf16[768,1024]{1,0:T(8,128)(2,1)} %collective-permute-done.2, bf16[768,1024]{1,0:T(8,128)(2,1)} %collective-permute-done.1, bf16[768,1024]{1,0:T(8,128)(2,1)} %collective-permute-done, bf16[768,1024]{1,0:T(8,128)(2,1)S(1)} %copy-done.15, bf16[768,768]{1,0:T(8,128)(2,1)S(1)} %copy-done.10, ...), kind=kOutput, calls=%fused_computation.121 | convolution fusion | flops 4876664832 | bytes 12582912 | tf_op jit(solution)/shard_map/dot_general | solution.py:20
  493.6 4.6 add_convert_fusion
  506.9 5.5 add_convert_fusion.1
  514.1 21.6 %collective-permute-done.23 = bf16[768,1024]{1,0:T(8,128)(2,1)S(1)} collective-permute-done((bf16[768,1024]{1,0:T(8,128)(2,1)}, bf16[768,1024]{1,0:T(8,128)(2,1)S(1)}, u32[]{:S(2)}, u32[]{:S(2)}) %collective-permute-start.23) | collective-permute-done | bytes 1572896 | tf_op jit(solution)/shard_map/ppermute | solution.py:47
  540.8 4.1 convert_reduce_fusion.3
  548.4 83.5 %all-reduce.5.cloned.1.call-done = f32[16,8,128]{2,1,0:T(8,128)} async-done(((f32[16,8,128]{2,1,0:T(8,128)}), f32[16,8,128]{2,1,0:T(8,128)}) %all-reduce.5.cloned.1.call-update) | async-done | bytes 65552
  634.6 5.5 add_add_fusion.3
  (320 shorter events, 133.6 us)
Async XLA Ops:
  7.2 91.4 %all-gather.4.cloned.1.call-start = ((), (), s32[]{:S(2)}) async-start(), calls=%async_computation.4 | async-start | bytes 1966080 | tf_op jit(solution)/shard_map/all_gather | solution.py:268
  9.3 205.0 %all-gather.6.cloned.1.call-start = ((), (), s32[]{:S(2)}) async-start(), calls=%async_computation.5 | async-start | bytes 2621440 | tf_op jit(solution)/shard_map/all_gather | solution.py:273
  39.9 36.8 %collective-permute-start.1 = (bf16[768,1024]{1,0:T(8,128)(2,1)S(1)}, bf16[768,1024]{1,0:T(8,128)(2,1)}, u32[]{:S(2)}, u32[]{:S(2)}) collective-permute-start(bf16[768,1024]{1,0:T(8,128)(2,1)S(1)} %fusion.46), channel_id=1, source_target_pairs={{0,2},{1,3},{2,0},{3,1},{4,6},{5,7},{6,4},{7,5},{8,10},{9,11},{10,... | collective-permute-start | bytes 4718600 | tf_op jit(solution)/shard_map/ppermute | solution.py:47
  40.0 61.7 %collective-permute-start = (bf16[768,1024]{1,0:T(8,128)(2,1)S(1)}, bf16[768,1024]{1,0:T(8,128)(2,1)}, u32[]{:S(2)}, u32[]{:S(2)}) collective-permute-start(bf16[768,1024]{1,0:T(8,128)(2,1)S(1)} %fusion.46), channel_id=1, source_target_pairs={{0,1},{1,0},{2,3},{3,2},{4,5},{5,4},{6,7},{7,6},{8,9},{9,8},{10,11... | collective-permute-start | bytes 4718600 | tf_op jit(solution)/shard_map/ppermute | solution.py:47
  40.4 206.7 %all-gather.8.cloned.1.call-start = ((), (), s32[]{:S(2)}) async-start(), calls=%async_computation.6 | async-start | bytes 2621440 | tf_op jit(solution)/shard_map/all_gather | solution.py:272
  76.7 30.7 %collective-permute-start.2 = (bf16[768,1024]{1,0:T(8,128)(2,1)}, bf16[768,1024]{1,0:T(8,128)(2,1)}, u32[]{:S(2)}, u32[]{:S(2)}) collective-permute-start(bf16[768,1024]{1,0:T(8,128)(2,1)} %collective-permute-done.1), channel_id=1, source_target_pairs={{0,1},{1,0},{2,3},{3,2},{4,5},{5,4},{6,7},{7,6},{8,9},{9,8},{10,11... | collective-permute-start | bytes 4718600 | tf_op jit(solution)/shard_map/ppermute | solution.py:47
  143.0 37.6 %collective-permute-start.5 = (bf16[768,1024]{1,0:T(8,128)(2,1)}, bf16[768,1024]{1,0:T(8,128)(2,1)}, u32[]{:S(2)}, u32[]{:S(2)}) collective-permute-start(bf16[768,1024]{1,0:T(8,128)(2,1)} %add_convert_fusion.4), channel_id=1, source_target_pairs={{0,2},{1,3},{2,0},{3,1},{4,6},{5,7},{6,4},{7,5},{8,10},{9,11},{10,... | collective-permute-start | bytes 4718600 | tf_op jit(solution)/shard_map/ppermute | solution.py:47
  143.8 207.0 %reduce-scatter.11.cloned.1.call-start = ((), (), s32[]{:S(2)}) async-start(), calls=%async_computation.10 | async-start | bytes 2621440 | tf_op jit(solution)/shard_map/reduce_scatter | solution.py:320
  145.6 68.6 %collective-permute-start.9 = (bf16[768,1024]{1,0:T(8,128)(2,1)}, bf16[768,1024]{1,0:T(8,128)(2,1)}, u32[]{:S(2)}, u32[]{:S(2)}) collective-permute-start(bf16[768,1024]{1,0:T(8,128)(2,1)} %param.27), channel_id=1, source_target_pairs={{0,2},{1,3},{2,0},{3,1},{4,6},{5,7},{6,4},{7,5},{8,10},{9,11},{10,... | collective-permute-start | bytes 4718600 | tf_op jit(solution)/shard_map/ppermute | solution.py:47
  146.9 78.5 %collective-permute-start.6 = (bf16[768,1024]{1,0:T(8,128)(2,1)}, bf16[768,1024]{1,0:T(8,128)(2,1)}, u32[]{:S(2)}, u32[]{:S(2)}) collective-permute-start(bf16[768,1024]{1,0:T(8,128)(2,1)} %param.27), channel_id=1, source_target_pairs={{0,1},{1,0},{2,3},{3,2},{4,5},{5,4},{6,7},{7,6},{8,9},{9,8},{10,11... | collective-permute-start | bytes 4718600 | tf_op jit(solution)/shard_map/ppermute | solution.py:47
  186.3 60.8 %collective-permute-start.10 = (bf16[768,1024]{1,0:T(8,128)(2,1)}, bf16[768,1024]{1,0:T(8,128)(2,1)}, u32[]{:S(2)}, u32[]{:S(2)}) collective-permute-start(bf16[768,1024]{1,0:T(8,128)(2,1)} %add_convert_fusion.3), channel_id=1, source_target_pairs={{0,2},{1,3},{2,0},{3,1},{4,6},{5,7},{6,4},{7,5},{8,10},{9,11},{10,... | collective-permute-start | bytes 4718600 | tf_op jit(solution)/shard_map/ppermute | solution.py:47
  214.3 36.9 %collective-permute-start.11 = (bf16[768,1024]{1,0:T(8,128)(2,1)}, bf16[768,1024]{1,0:T(8,128)(2,1)}, u32[]{:S(2)}, u32[]{:S(2)}) collective-permute-start(bf16[768,1024]{1,0:T(8,128)(2,1)} %collective-permute-done.9), channel_id=1, source_target_pairs={{0,1},{1,0},{2,3},{3,2},{4,5},{5,4},{6,7},{7,6},{8,9},{9,8},{10,11... | collective-permute-start | bytes 4718600 | tf_op jit(solution)/shard_map/ppermute | solution.py:47
  224.9 34.6 %collective-permute-start.7 = (bf16[768,1024]{1,0:T(8,128)(2,1)}, bf16[768,1024]{1,0:T(8,128)(2,1)}, u32[]{:S(2)}, u32[]{:S(2)}) collective-permute-start(bf16[768,1024]{1,0:T(8,128)(2,1)} %add_convert_fusion.3), channel_id=1, source_target_pairs={{0,1},{1,0},{2,3},{3,2},{4,5},{5,4},{6,7},{7,6},{8,9},{9,8},{10,11... | collective-permute-start | bytes 4718600 | tf_op jit(solution)/shard_map/ppermute | solution.py:47
  247.1 15.7 %collective-permute-start.12 = (bf16[768,1024]{1,0:T(8,128)(2,1)}, bf16[768,1024]{1,0:T(8,128)(2,1)}, u32[]{:S(2)}, u32[]{:S(2)}) collective-permute-start(bf16[768,1024]{1,0:T(8,128)(2,1)} %collective-permute-done.10), channel_id=1, source_target_pairs={{0,1},{1,0},{2,3},{3,2},{4,5},{5,4},{6,7},{7,6},{8,9},{9,8},{10,11... | collective-permute-start | bytes 4718600 | tf_op jit(solution)/shard_map/ppermute | solution.py:47
  290.6 100.5 %reduce-scatter.9.cloned.1.call-start = ((), (), s32[]{:S(2)}) async-start(), calls=%async_computation.9 | async-start | bytes 2621440 | tf_op jit(solution)/shard_map/reduce_scatter | solution.py:320
  298.5 20.3 %collective-permute-start.8 = (bf16[768,1024]{1,0:T(8,128)(2,1)}, bf16[768,1024]{1,0:T(8,128)(2,1)}, u32[]{:S(2)}, u32[]{:S(2)}) collective-permute-start(bf16[768,1024]{1,0:T(8,128)(2,1)} %convolution_convert_fusion.5), channel_id=1, source_target_pairs={{0,1},{1,0},{2,3},{3,2},{4,5},{5,4},{6,7},{7,6},{8,9},{9,8},{10,11... | collective-permute-start | bytes 4718600 | tf_op jit(solution)/shard_map/ppermute | solution.py:47
  301.6 37.1 %collective-permute-start.14 = (bf16[768,1024]{1,0:T(8,128)(2,1)}, bf16[768,1024]{1,0:T(8,128)(2,1)}, u32[]{:S(2)}, u32[]{:S(2)}) collective-permute-start(bf16[768,1024]{1,0:T(8,128)(2,1)} %add_convert_fusion.2), channel_id=1, source_target_pairs={{0,2},{1,3},{2,0},{3,1},{4,6},{5,7},{6,4},{7,5},{8,10},{9,11},{10,... | collective-permute-start | bytes 4718600 | tf_op jit(solution)/shard_map/ppermute | solution.py:47
  314.4 190.7 %reduce-scatter.7.cloned.1.call-start = ((), (), s32[]{:S(2)}) async-start(), calls=%async_computation.8 | async-start | bytes 655360 | tf_op jit(solution)/shard_map/reduce_scatter | solution.py:320
  348.1 36.2 %collective-permute-start.16 = (bf16[768,1024]{1,0:T(8,128)(2,1)}, bf16[768,1024]{1,0:T(8,128)(2,1)}, u32[]{:S(2)}, u32[]{:S(2)}) collective-permute-start(bf16[768,1024]{1,0:T(8,128)(2,1)} %get-tuple-element.104), channel_id=1, source_target_pairs={{0,2},{1,3},{2,0},{3,1},{4,6},{5,7},{6,4},{7,5},{8,10},{9,11},{10,... | collective-permute-start | bytes 4718600 | tf_op jit(solution)/shard_map/ppermute | solution.py:47
  348.9 58.3 %collective-permute-start.15 = (bf16[768,1024]{1,0:T(8,128)(2,1)}, bf16[768,1024]{1,0:T(8,128)(2,1)}, u32[]{:S(2)}, u32[]{:S(2)}) collective-permute-start(bf16[768,1024]{1,0:T(8,128)(2,1)} %get-tuple-element.104), channel_id=1, source_target_pairs={{0,1},{1,0},{2,3},{3,2},{4,5},{5,4},{6,7},{7,6},{8,9},{9,8},{10,11... | collective-permute-start | bytes 4718600 | tf_op jit(solution)/shard_map/ppermute | solution.py:47
  350.8 44.5 %collective-permute-start.28 = (bf16[1024,256]{1,0:T(8,128)(2,1)}, bf16[1024,256]{1,0:T(8,128)(2,1)}, u32[]{:S(2)}, u32[]{:S(2)}) collective-permute-start(bf16[1024,256]{1,0:T(8,128)(2,1)} %reduce-scatter.11.cloned.1.call-done), channel_id=1, source_target_pairs={{0,16},{16,0},{1,17},{17,1},{2,18},{18,2},{3,19},{19,3},{4,20},{20... | collective-permute-start | bytes 1572872 | tf_op jit(solution)/shard_map/ppermute | solution.py:101
  384.4 27.0 %collective-permute-start.17 = (bf16[768,1024]{1,0:T(8,128)(2,1)}, bf16[768,1024]{1,0:T(8,128)(2,1)}, u32[]{:S(2)}, u32[]{:S(2)}) collective-permute-start(bf16[768,1024]{1,0:T(8,128)(2,1)} %collective-permute-done.16), channel_id=1, source_target_pairs={{0,1},{1,0},{2,3},{3,2},{4,5},{5,4},{6,7},{7,6},{8,9},{9,8},{10,11... | collective-permute-start | bytes 4718600 | tf_op jit(solution)/shard_map/ppermute | solution.py:47
  416.0 130.7 %reduce-scatter.5.cloned.1.call-start = ((), (), s32[]{:S(2)}) async-start(), calls=%async_computation.7 | async-start | bytes 1966080 | tf_op jit(solution)/shard_map/reduce_scatter | solution.py:320
  467.1 26.4 %collective-permute-start.22 = (bf16[768,1024]{1,0:T(8,128)(2,1)}, bf16[768,1024]{1,0:T(8,128)(2,1)}, u32[]{:S(2)}, u32[]{:S(2)}) collective-permute-start(bf16[768,1024]{1,0:T(8,128)(2,1)} %convolution_convert_fusion), channel_id=1, source_target_pairs={{0,1},{1,0},{2,3},{3,2},{4,5},{5,4},{6,7},{7,6},{8,9},{9,8},{10,11... | collective-permute-start | bytes 4718600 | tf_op jit(solution)/shard_map/ppermute | solution.py:47
  469.7 44.4 %collective-permute-start.21 = (bf16[768,1024]{1,0:T(8,128)(2,1)}, bf16[768,1024]{1,0:T(8,128)(2,1)}, u32[]{:S(2)}, u32[]{:S(2)}) collective-permute-start(bf16[768,1024]{1,0:T(8,128)(2,1)} %convolution_convert_fusion.1), channel_id=1, source_target_pairs={{0,1},{1,0},{2,3},{3,2},{4,5},{5,4},{6,7},{7,6},{8,9},{9,8},{10,11... | collective-permute-start | bytes 4718600 | tf_op jit(solution)/shard_map/ppermute | solution.py:47
  481.0 25.9 %collective-permute-start.19 = (bf16[768,1024]{1,0:T(8,128)(2,1)}, bf16[768,1024]{1,0:T(8,128)(2,1)}, u32[]{:S(2)}, u32[]{:S(2)}) collective-permute-start(bf16[768,1024]{1,0:T(8,128)(2,1)} %convolution_convert_fusion.2), channel_id=1, source_target_pairs={{0,1},{1,0},{2,3},{3,2},{4,5},{5,4},{6,7},{7,6},{8,9},{9,8},{10,11... | collective-permute-start | bytes 4718600 | tf_op jit(solution)/shard_map/ppermute | solution.py:47
  484.0 150.6 %collective-permute-start.18 = (bf16[768,1024]{1,0:T(8,128)(2,1)}, bf16[768,1024]{1,0:T(8,128)(2,1)}, u32[]{:S(2)}, u32[]{:S(2)}) collective-permute-start(bf16[768,1024]{1,0:T(8,128)(2,1)} %convolution_convert_fusion.3), channel_id=1, source_target_pairs={{0,1},{1,0},{2,3},{3,2},{4,5},{5,4},{6,7},{7,6},{8,9},{9,8},{10,11... | collective-permute-start | bytes 4718600 | tf_op jit(solution)/shard_map/ppermute | solution.py:47
  493.2 138.6 %all-reduce.5.cloned.1.call-start = ((), (), s32[]{:S(2)}) async-start(), calls=%async_computation.11 | async-start | bytes 131072
  498.1 37.5 %collective-permute-start.23 = (bf16[768,1024]{1,0:T(8,128)(2,1)}, bf16[768,1024]{1,0:T(8,128)(2,1)S(1)}, u32[]{:S(2)}, u32[]{:S(2)}) collective-permute-start(bf16[768,1024]{1,0:T(8,128)(2,1)} %add_convert_fusion), channel_id=1, source_target_pairs={{0,2},{1,3},{2,0},{3,1},{4,6},{5,7},{6,4},{7,5},{8,10},{9,11},{10,... | collective-permute-start | bytes 4718600 | tf_op jit(solution)/shard_map/ppermute | solution.py:47
  505.2 40.8 %collective-permute-start.26 = (bf16[256,256]{1,0:T(8,128)(2,1)}, bf16[256,256]{1,0:T(8,128)(2,1)S(1)}, u32[]{:S(2)}, u32[]{:S(2)}) collective-permute-start(bf16[256,256]{1,0:T(8,128)(2,1)} %reduce-scatter.7.cloned.1.call-done), channel_id=1, source_target_pairs={{0,16},{16,0},{1,17},{17,1},{2,18},{18,2},{3,19},{19,3},{4,20},{20... | collective-permute-start | bytes 393224 | tf_op jit(solution)/shard_map/ppermute | solution.py:101
  512.4 122.2 %collective-permute-start.20 = (bf16[768,1024]{1,0:T(8,128)(2,1)}, bf16[768,1024]{1,0:T(8,128)(2,1)}, u32[]{:S(2)}, u32[]{:S(2)}) collective-permute-start(bf16[768,1024]{1,0:T(8,128)(2,1)} %add_convert_fusion.1), channel_id=1, source_target_pairs={{0,2},{1,3},{2,0},{3,1},{4,6},{5,7},{6,4},{7,5},{8,10},{9,11},{10,... | collective-permute-start | bytes 4718600 | tf_op jit(solution)/shard_map/ppermute | solution.py:47
  546.7 96.8 %collective-permute-start.25 = (bf16[256,768]{1,0:T(8,128)(2,1)}, bf16[256,768]{1,0:T(8,128)(2,1)}, u32[]{:S(2)}, u32[]{:S(2)}) collective-permute-start(bf16[256,768]{1,0:T(8,128)(2,1)} %reduce-scatter.5.cloned.1.call-done), channel_id=1, source_target_pairs={{0,16},{16,0},{1,17},{17,1},{2,18},{18,2},{3,19},{19,3},{4,20},{20... | collective-permute-start | bytes 1179656 | tf_op jit(solution)/shard_map/ppermute | solution.py:101
  (72 other events, 1176.6 us)
Sparse Core Ops, SparseCore 0:
  10.1 40.4 all-gather.3
  52.2 52.9 all-gather.5
  143.9 45.9 all-gather.7
  290.7 43.7 reduce-scatter.10
  337.2 42.8 reduce-scatter.8
  416.2 21.3 reduce-scatter.6
  493.4 34.8 reduce-scatter.4
  546.1 85.7 all-reduce.4
